TPU v7x, 128 devices: a whole 4x4x4 slice. The times are simulated.
128 devices in a mesh: dp: 64 (over z, y, x), vocab: 2 (over core).
Axes of the slice: x: 4, y: 4, z: 4, core: 2. Of those that a mesh axis runs over, the one named last changes fastest.
Arguments:
- hidden_states: bfloat16 [1024, 3584], P('dp'), may hold values from -400 to 400
- targets: int32 [1024], P('dp'), may hold values from 0 to 196607
- out_weight: bfloat16 [3584, 196608], P(None, ('dp', 'vocab')), may hold values from -5 to 5
Outputs:
- token_loss: float32 [1024], P('dp')
- loss_mean: float32 [], replicated
All inputs are finite; a program needn't handle non-finite values.
Results may differ from a plain program's by a relative error of at most 0.0003.
Values may be sent and summed in bfloat16 or wider, within the bound.
A program may use at most 64 MiB of HBM per device.

v0:
```python
import jax
import jax.numpy as jnp
from jax import lax
from jax.sharding import Mesh
from jax.sharding import PartitionSpec as P

DP = ("dp_0", "dp_1", "dp_2")
DP_VOCAB = ("dp_0", "dp_1", "dp_2", "vocab")


def collected_together(x, axis):
    leaves = jax.tree.leaves(x)
    order = sorted(range(len(leaves)), key=lambda k: -leaves[k].size)
    width = (1, *leaves[order[0]].shape)[-1]
    lines = [
        jnp.pad(leaves[k].reshape(-1), (0, -leaves[k].size % width)).reshape(-1, width)
        for k in order
    ]
    both, at, found = (lax.all_gather(jnp.concatenate(lines), axis), 0, {})
    for k, line in zip(order, lines):
        slab = both[:, at : at + len(line)].reshape(len(both), -1)
        found[k] = slab[:, : leaves[k].size].reshape(-1, *leaves[k].shape)
        at += len(line)
    numbers = iter(range(len(leaves)))
    return jax.tree.map(lambda _: found[next(numbers)], x)


def joined_all(x, axes, combine):
    for axis in axes:
        pieces = collected_together(x, axis)
        x = jax.tree.map(lambda part: part[0], pieces)
        for k in range(1, lax.axis_size(axis)):
            x = combine(x, jax.tree.map(lambda part: part[k], pieces))
    return x


def shards(hidden_states, targets, out_weight):
    vocab_cols = out_weight.shape[1]
    local_tokens = hidden_states.shape[0]
    pairs = lax.axis_size("vocab")
    states, labels = (
        lax.all_gather(hidden_states, DP, axis=0, tiled=True),
        lax.all_gather(targets, DP, axis=0, tiled=True),
    )
    logits = jnp.dot(states, out_weight, preferred_element_type=jnp.float32)
    start = (lax.axis_index(DP) * pairs + lax.axis_index("vocab")) * vocab_cols
    columns = start + lax.broadcasted_iota(jnp.int32, logits.shape, 1)
    is_target = columns == labels[:, None]
    picked = jnp.sum(jnp.where(is_target, logits, 0.0), axis=1)
    local_top = jnp.max(logits, axis=1)
    exp_local = jnp.sum(jnp.exp(logits - local_top[:, None]), axis=1)

    def combine(earlier, later):
        highest = jnp.maximum(earlier[0], later[0])
        scaled = earlier[1] * jnp.exp(earlier[0] - highest) + later[1] * jnp.exp(later[0] - highest)
        return (highest, scaled, earlier[2] + later[2])

    row_top, exp_total, target_logit = joined_all((local_top, exp_local, picked), DP_VOCAB, combine)
    all_loss = row_top + jnp.log(exp_total) - target_logit
    token_loss = lax.dynamic_slice_in_dim(
        all_loss, lax.axis_index(DP) * local_tokens, local_tokens, 0
    )
    loss_mean = jnp.mean(all_loss)
    return (token_loss, loss_mean)


def solution(mesh):
    torus = Mesh(
        mesh.devices.reshape(4, 4, 4, mesh.shape["vocab"]), ("dp_0", "dp_1", "dp_2", "vocab")
    )
    placed = (P(DP, None), P(DP), P(None, DP_VOCAB))
    return jax.shard_map(
        shards, mesh=torus, in_specs=placed, out_specs=(P(DP), P()), check_vma=False
    )
```

profile of v0, /device:TPU:0, one launch (start us, length us, event | category | flops | bytes accessed | tf_op | source)
XLA Modules:
  0.0 155.6 jit_solution(10694057390076356137)
XLA Ops:
  7.2 0.0 all-gather.10.cloned.1.call-start
  7.2 0.7 all-gather.10.cloned.1.call-update
  7.9 1.2 dynamic-slice
  9.8 0.9 dynamic-update-slice
  10.7 25.4 %all-reduce = s32[1024]{0:T(1024)S(1)} all-reduce(s32[1024]{0:T(1024)S(1)} %dynamic-update-slice), channel_id=1, replica_groups=mesh['dp_0'=4,'dp_1'=4,'dp_2'=4,'vocab'=2] {'dp_0','dp_1','dp_2'}, use_global_device_ids=true, to_apply=%add | all-reduce | flops 1024 | bytes 8192
  36.1 52.3 %all-gather.10.cloned.1.call-done = bf16[1024,3584]{1,0:T(8,128)(2,1)} async-done(((bf16[16,3584]{1,0:T(8,128)(2,1)}), bf16[1024,3584]{1,0:T(8,128)(2,1)}) %all-gather.10.cloned.1.call-update) | async-done | bytes 7340048 | tf_op jit(solution)/shard_map/all_gather | solution.py:42
  88.4 16.8 %fusion.46 = (f32[1024]{0:T(1024)S(1)}, f32[1024,1536]{1,0:T(8,128)S(1)}) fusion(bf16[1024,3584]{1,0:T(8,128)(2,1)} %all-gather.10.cloned.1.call-done, bf16[3584,1536]{1,0:T(8,128)(2,1)} %param.5), kind=kOutput, calls=%fused_computation.86 | convolution fusion | flops 11275860992 | bytes 24645632 | tf_op jit(solution)/shard_map/dot_general | solution.py:45
  105.2 2.1 %exponential_reduce_fusion = (f32[1024]{0:T(1024)S(1)}, f32[1024]{0:T(1024)S(1)}) fusion(f32[1024,1536]{1,0:T(8,128)S(1)} %get-tuple-element.18, f32[1024]{0:T(1024)S(1)} %get-tuple-element.17, s32[1024]{0:T(1024)S(1)} %all-reduce, s32[1536]{0:T(1024)S(1)} %iota_add_fusion), kind=kLoop, calls=%fused_computation.1 | loop fusion | flops 7862272 | bytes 6313984 | tf_op jit(solution)/shard_map/reduce_sum | solution.py:51
  107.3 11.9 %all-gather.4 = f32[4,3,1024]{2,1,0:T(4,128)S(1)} all-gather(f32[1,3,1024]{2,1,0:T(4,128)S(1)} %maximum_bitcast_fusion), channel_id=2, replica_groups=mesh['dp_0'=4,'dp_1'=4,'dp_2'=4,'vocab'=2] {'dp_0'}, dimensions={0}, use_global_device_ids=true | all-gather | bytes 61440 | tf_op jit(solution)/shard_map/all_gather | solution.py:19
  119.2 0.1 fusion.22
  119.3 12.2 %all-gather.5 = f32[4,3,1024]{2,1,0:T(4,128)S(1)} all-gather(f32[1,3,1024]{2,1,0:T(4,128)S(1)} %maximum_bitcast_fusion.1), channel_id=3, replica_groups=mesh['dp_0'=4,'dp_1'=4,'dp_2'=4,'vocab'=2] {'dp_1'}, dimensions={0}, use_global_device_ids=true | all-gather | bytes 61440 | tf_op jit(solution)/shard_map/all_gather | solution.py:19
  131.5 0.1 fusion.12
  131.6 12.2 %all-gather.6 = f32[4,3,1024]{2,1,0:T(4,128)S(1)} all-gather(f32[1,3,1024]{2,1,0:T(4,128)S(1)} %maximum_bitcast_fusion.2), channel_id=4, replica_groups=mesh['dp_0'=4,'dp_1'=4,'dp_2'=4,'vocab'=2] {'dp_2'}, dimensions={0}, use_global_device_ids=true | all-gather | bytes 61440 | tf_op jit(solution)/shard_map/all_gather | solution.py:19
  143.8 0.1 fusion.2
  143.9 1.8 %all-gather.7 = f32[2,3,1024]{2,1,0:T(4,128)S(1)} all-gather(f32[1,3,1024]{2,1,0:T(4,128)S(1)} %maximum_bitcast_fusion.3), channel_id=5, replica_groups=mesh['dp_0'=4,'dp_1'=4,'dp_2'=4,'vocab'=2] {'vocab'}, dimensions={0}, use_global_device_ids=true | all-gather | bytes 36864 | tf_op jit(solution)/shard_map/all_gather | solution.py:19
  145.7 0.6 fusion.41
  146.4 0.6 dynamic_slice.3
  (10 shorter events, 0.1 us)
Async XLA Ops:
  7.2 81.3 %all-gather.10.cloned.1.call-start = ((), (), s32[]{:S(2)}) async-start(), calls=%async_computation | async-start | bytes 7454720 | tf_op jit(solution)/shard_map/all_gather | solution.py:42
Sparse Core Ops, SparseCore 0:
  10.7 77.6 all-gather.9
where the time goes:
time: 157 us; the launch traced here: 156 us
  blocking collectives  63.5 us (40%)
  waiting for transfers between devices  53 us (34%)
  matrix products  16.8 us (11%)
  between operations  16.6 us (11%)
  other arithmetic  3.02 us (2%)
  local copies, waits for them, and re-layouts  2.69 us (2%)
    all_gather x1, waiting for transfers between devices, shards(): lax.all_gather(hidden_states, DP, axis=0, tiled=True)  52.3 us
    all_gather x4, blocking collectives, collected_together(): both, at, found = (lax.all_gather(jnp.concatenate(lines), axis), 0, {})  38.1 us
    unnamed x1, blocking collectives  25.4 us
    dot_general x1, matrix products, shards(): logits = jnp.dot(states, out_weight, preferred_element_type=jnp.float32)  16.8 us
  transfers between devices with their start and end apart: 1, of which 1 were waited for; matrix products, arithmetic and copies ran while one was open for 1% of the time, Pallas kernels for 0%

commit v1 on v0

v1 whole, which is shorter than its diff:
```python
import functools

import jax
import jax.numpy as jnp
from jax import lax
from jax.experimental import pallas as pl
from jax.experimental.pallas import tpu as pltpu
from jax.sharding import Mesh
from jax.sharding import PartitionSpec as P

MESH = pl.DeviceIdType.MESH
AXES = ("dp_0", "dp_1", "dp_2", "vocab")
DP = AXES[:3]

WIDTHS = (768, 512, 512)
STARTS = (0, 768, 1280)
HALF = 1792
ROWS = (
    (0, 0), (0, 1), (0, 2), (0, 3),
    (3, 0), (1, 0),
    (3, 1), (1, 3),
    (2, 0), (1, 2),
    (3, 2), (2, 3),
    (2, 1), (2, 2),
    (3, 3), (1, 1),
)
SLOT = {row: i for i, row in enumerate(ROWS)}
NT = 512


def kernel(h_ref, t_ref, w_ref, loss_ref, mean_ref, *scratch):
    own, part = scratch[0:3], scratch[3:6]
    (w, acc, tg, tsm, stats, lanes, parts, line,
     a_send, a_recv, b_send, b_recv, c_send, c_recv, p_send, p_recv,
     t_send, t_recv, s_send, s_recv, local, wsem) = scratch[6:]
    pos = tuple(lax.axis_index(name) for name in DP)
    core = lax.axis_index("vocab")
    chip = pos[0] * 16 + pos[1] * 4 + pos[2]
    vocab_cols = w.shape[1]

    def turn(h, dim, k):
        return (1 - h) * int(dim % 3 == k) + h * int((dim + 1) % 3 == k)

    def moved(dim, step):
        return tuple(lax.rem(pos[k] + step * turn(core, dim, k), 4) for k in range(3)) + (core,)

    def along(k, step):
        return tuple(lax.rem(pos[i] + (step if i == k else 0), 4) for i in range(3)) + (core,)

    partner = pos + (1 - core,)

    loads = []
    for j in range(3):
        for k, (buf, h) in enumerate(((own[j], core), (part[j], 1 - core))):
            cols = pl.ds(pl.multiple_of(h * HALF + STARTS[j], 256), WIDTHS[j])
            loads.append(
                pltpu.make_async_copy(h_ref.at[:, cols], buf.at[pl.ds(0, 16)], local.at[2 * j + k])
            )
    loads.append(pltpu.make_async_copy(t_ref, tsm, local.at[6]))
    for copy in loads:
        copy.start()
    pieces = wsem.shape[0]
    deep = w.shape[0] // pieces
    wloads = [
        pltpu.make_async_copy(
            w_ref.at[pl.ds(i * deep, deep)], w.at[pl.ds(i * deep, deep)], wsem.at[i]
        )
        for i in range(pieces)
    ]
    for copy in wloads:
        copy.start()

    barrier = pltpu.get_barrier_semaphore()
    peers = [partner] + [along(k, s) for k in range(3) for s in (1, 2, 3)]
    for peer in peers:
        pl.semaphore_signal(barrier, inc=1, device_id=peer, device_id_type=MESH)
    pl.semaphore_wait(barrier, len(peers))

    def remote(src, dst, send, recv, device):
        return pltpu.make_async_remote_copy(
            src_ref=src, dst_ref=dst, send_sem=send, recv_sem=recv,
            device_id=device, device_id_type=MESH,
        )

    def block(buf, slot, n=1):
        return buf.at[pl.ds(slot * 64, n * 64)]

    def a_copy(j, s):
        return remote(
            own[j].at[pl.ds(0, 16)], own[j].at[pl.ds((4 - s) * 16, 16)],
            a_send.at[j, s - 1], a_recv.at[j, 3 - s], moved(j + 2, s),
        )

    def b_copy(j, s):
        return remote(
            block(own[j], 0), block(own[j], 4 - s),
            b_send.at[j, s - 1], b_recv.at[j, 3 - s], moved(j + 1, s),
        )

    def c_copy(j, rc, rb, s):
        src, dst = SLOT[rc, rb], SLOT[(rc - s) % 4, rb]
        return remote(
            block(own[j], src), block(own[j], dst),
            c_send.at[j, dst - 4], c_recv.at[j, dst - 4], moved(j, s),
        )

    def c_wait(j, slot):
        remote(
            block(own[j], slot), block(own[j], slot),
            c_send.at[j, slot - 4], c_recv.at[j, slot - 4], partner,
        ).wait_recv()

    def p_copy(j, k):
        start, size = ((16, 48), (64, 192))[k] if k < 2 else (k * 128, 128)
        return remote(
            own[j].at[pl.ds(start, size)], part[j].at[pl.ds(start, size)],
            p_send.at[j, k], p_recv.at[j, k], partner,
        )

    def t_copy(k, s):
        n = 4 ** (2 - k)
        rows = pl.ds(chip // n * n, n)
        return remote(
            tg.at[rows], tg.at[rows], t_send.at[k, s - 1], t_recv.at[k, 3 - s], along(k, s)
        )

    def t_wait(k, r):
        n = 4 ** (2 - k)
        other = sum(
            (lax.rem(pos[i] + r, 4) if i == k else pos[i]) * (16, 4, 1)[i] for i in range(3)
        )
        rows = pl.ds(other // n * n, n)
        remote(
            tg.at[rows], tg.at[rows], t_send.at[k, 0], t_recv.at[k, r - 1], partner
        ).wait_recv()

    for copy in loads:
        copy.wait()
    for j in range(3):
        for s in (1, 3, 2):
            a_copy(j, s).start()
    spots = lax.broadcasted_iota(jnp.int32, (1, 128), 1) - lax.rem(chip, 8) * 16
    mine = jnp.zeros((1, 128), jnp.int32)
    for i in range(16):
        mine = jnp.where(spots == i, tsm[i], mine)
    tg[chip] = mine
    acc[...] = jnp.zeros_like(acc)
    for s in (1, 3, 2):
        t_copy(2, s).start()

    for j in range(3):
        for r in (1, 3, 2):
            a_copy(j, 4 - r).wait_recv()
        for s in (1, 3, 2):
            b_copy(j, s).start()
        for s in (1, 3):
            c_copy(j, 0, 0, s).start()
        p_copy(j, 0).start()
    for r in (1, 2, 3):
        t_wait(2, r)
    for s in (1, 3, 2):
        t_copy(1, s).start()
    for copy in wloads:
        copy.wait()

    def pair(p):
        def entry(i, which):
            return sum(ROWS[2 * k + i][which] * (p == k).astype(jnp.int32) for k in range(8))

        rel = [(entry(i, 0), entry(i, 1)) for i in range(2)]
        for bufs, h in ((own, core), (part, 1 - core)):
            for j in range(3):
                spread = []
                for i in range(8):
                    rc, rb = rel[i // 4]
                    place = 0
                    for k in range(3):
                        shift = rc * turn(h, j, k) + rb * turn(h, j + 1, k)
                        shift = shift + (i % 4) * turn(h, j + 2, k)
                        place = place * 4 + lax.rem(pos[k] + shift, 4)
                    spread.append(pl.multiple_of(place * 16, 16))
                lhs = bufs[j][pl.ds(pl.multiple_of(p * 128, 128), 128), :]
                rows = pl.ds(pl.multiple_of(h * HALF + STARTS[j], 256), WIDTHS[j])
                for n in range(vocab_cols // NT):
                    cols = pl.ds(n * NT, NT)
                    out = jnp.dot(lhs, w[rows, cols], preferred_element_type=jnp.float32)
                    for i in range(8):
                        acc[pl.ds(spread[i], 16), cols] += out[16 * i : 16 * i + 16]

    def step(p, carry):
        @pl.when(p == 0)
        def _():
            for j in range(3):
                for r in (1, 3, 2):
                    b_copy(j, 4 - r).wait_recv()
                c_copy(j, 0, 1, 1).start()
                c_copy(j, 0, 3, 3).start()
                c_copy(j, 0, 2, 3).start()
                p_copy(j, 1).start()
            for j in range(3):
                p_copy(j, 0).wait_recv()
                p_copy(j, 1).wait_recv()

        for k in range(1, 7):

            @pl.when(p == k)
            def _(k=k):
                for j in range(3):
                    c_wait(j, 2 * k + 2)
                    c_wait(j, 2 * k + 3)
                    if k == 1:
                        c_copy(j, 3, 0, 1).start()
                        c_copy(j, 0, 2, 1).start()
                    if k == 2:
                        c_copy(j, 3, 1, 1).start()
                        c_copy(j, 1, 3, 3).start()
                        c_copy(j, 0, 3, 1).start()
                    if k == 3:
                        c_copy(j, 1, 2, 3).start()
                        c_copy(j, 0, 1, 3).start()
                    p_copy(j, k + 1).start()
                if k == 1:
                    for r in (1, 2, 3):
                        t_wait(1, r)
                    for s in (1, 3, 2):
                        t_copy(0, s).start()

        for k in range(2, 8):

            @pl.when(p == k)
            def _(k=k):
                for j in range(3):
                    p_copy(j, k).wait_recv()

        pair(p)
        return carry

    lax.fori_loop(0, 8, step, 0)
    for r in (1, 2, 3):
        t_wait(0, r)

    first = (chip * 2 + core) * vocab_cols
    lane = lax.broadcasted_iota(jnp.int32, (128, 128), 1).astype(jnp.float32)
    base = lane + first.astype(jnp.float32)

    def tokens(i, carry):
        wanted = jnp.zeros((1, 128), jnp.int32)
        for k in range(8):
            wanted = wanted + tg[i * 8 + k]
        line[...] = jnp.broadcast_to(wanted.astype(jnp.float32), (128, 128)).T - base
        for half in range(2):
            rows = pl.ds(pl.multiple_of(i * 128 + half * 64, 64), 64)
            there = pl.ds(half * 64, 64)
            top = acc[rows, 0:128]
            for n in range(1, vocab_cols // 128):
                top = jnp.maximum(top, acc[rows, n * 128 : n * 128 + 128])
            total = jnp.zeros((64, 128), jnp.float32)
            hit = jnp.zeros((64, 128), jnp.float32)
            ahead = line[there, :]
            for n in range(vocab_cols // 128):
                x = acc[rows, n * 128 : n * 128 + 128]
                total = total + jnp.exp(x - top)
                hit = hit + jnp.where(ahead == float(n * 128), x, 0.0)
            lanes[0, there, :] = top
            lanes[1, there, :] = total
            lanes[2, there, :] = hit
        top = lanes[0].T
        best = jnp.max(top, axis=0, keepdims=True)
        stats[0, 0, pl.ds(i, 1), :] = best
        stats[0, 1, pl.ds(i, 1), :] = jnp.sum(lanes[1].T * jnp.exp(top - best), axis=0, keepdims=True)
        stats[0, 2, pl.ds(i, 1), :] = jnp.sum(lanes[2].T, axis=0, keepdims=True)
        return carry

    lax.fori_loop(0, 8, tokens, 0)

    def joined(found):
        top = functools.reduce(jnp.maximum, [f[0] for f in found])
        total = sum(f[1] * jnp.exp(f[0] - top) for f in found)
        return top, total, sum(f[2] for f in found)

    now = tuple(stats[0, k] for k in range(3))
    for phase, (axis, size) in enumerate(((3, 2), (2, 4), (1, 4), (0, 4))):
        at = core if axis == 3 else pos[axis]
        for k in range(3):
            parts[phase, at, k] = now[k]
        copies = []
        for s in range(1, size):
            to = partner if axis == 3 else along(axis, s)
            copies.append(
                remote(
                    parts.at[phase, at], parts.at[phase, at],
                    s_send.at[phase, s - 1], s_recv.at[phase, size - 1 - s], to,
                )
            )
            copies[-1].start()
        for s in range(1, size):
            other = lax.rem(at + s, size)
            remote(
                parts.at[phase, other], parts.at[phase, other],
                s_send.at[phase, s - 1], s_recv.at[phase, s - 1], partner,
            ).wait_recv()
        now = joined([tuple(parts[phase, q, k] for k in range(3)) for q in range(size)])
        for copy in copies:
            copy.wait_send()
    loss = now[0] + jnp.log(now[1]) - now[2]
    mean_ref[0, 0] = jnp.sum(loss) / loss.size
    stats[0, 0] = loss
    row = stats[0, 0, pl.ds(chip // 8, 1), :]
    row = pltpu.roll(row, lax.rem(128 - lax.rem(chip, 8) * 16, 128), 1)
    loss_ref[...] = row[:, 0:16]

    for j in range(3):
        for s in (1, 2, 3):
            a_copy(j, s).wait_send()
            b_copy(j, s).wait_send()
        for slot in range(4, 16):
            remote(
                block(own[j], slot), block(own[j], slot),
                c_send.at[j, slot - 4], c_recv.at[j, slot - 4], partner,
            ).wait_send()
        for k in range(8):
            p_copy(j, k).wait_send()
    for k in range(3):
        for s in (1, 2, 3):
            t_copy(k, s).wait_send()


def shards(hidden_states, targets, out_weight):
    depth, cols = out_weight.shape
    dma = pltpu.SemaphoreType.DMA
    loss, mean = pl.pallas_call(
        kernel,
        out_shape=(
            jax.ShapeDtypeStruct((1, 16), jnp.float32),
            jax.ShapeDtypeStruct((1, 1), jnp.float32),
        ),
        in_specs=[pl.BlockSpec(memory_space=pl.ANY)] * 3,
        out_specs=(
            pl.BlockSpec(memory_space=pltpu.VMEM),
            pl.BlockSpec(memory_space=pltpu.SMEM),
        ),
        scratch_shapes=[pltpu.VMEM((1024, n), jnp.bfloat16) for n in WIDTHS + WIDTHS]
        + [
            pltpu.VMEM((depth, cols), jnp.bfloat16),
            pltpu.VMEM((1024, cols), jnp.float32),
            pltpu.VMEM((64, 1, 128), jnp.int32),
            pltpu.SMEM((16,), jnp.int32),
            pltpu.VMEM((1, 3, 8, 128), jnp.float32),
            pltpu.VMEM((3, 128, 128), jnp.float32),
            pltpu.VMEM((4, 4, 3, 8, 128), jnp.float32),
            pltpu.VMEM((128, 128), jnp.float32),
            dma((3, 3)), dma((3, 3)), dma((3, 3)), dma((3, 3)),
            dma((3, 12)), dma((3, 12)), dma((3, 8)), dma((3, 8)),
            dma((3, 3)), dma((3, 3)), dma((4, 3)), dma((4, 3)),
            dma((7,)), dma((7,)),
        ],
        compiler_params=pltpu.CompilerParams(
            collective_id=0, has_side_effects=True, vmem_limit_bytes=60 * 2**20
        ),
        name="score",
    )(hidden_states, targets, out_weight)
    return loss.reshape(16), mean.reshape(())


def solution(mesh):
    torus = Mesh(mesh.devices.reshape(4, 4, 4, mesh.shape["vocab"]), AXES)
    return jax.shard_map(
        shards, mesh=torus, in_specs=(P(DP, None), P(DP), P(None, AXES)), out_specs=(P(DP), P()), check_vma=False
    )
```

time: 157 us -> 56.4 us (0.36)
  blocking collectives: 63.5 us -> 0 us
  waiting for transfers between devices: 53 us -> 0 us
  Pallas kernels: 0 us -> 52.8 us
  matrix products: 16.8 us -> 0 us
  between operations: 16.6 us -> 2.4 us
  other arithmetic: 3.02 us -> 0 us
  local copies, waits for them, and re-layouts: 2.69 us -> 1.11 us
    pallas_call x0 -> x1, Pallas kernels: none -> 52.8 us  [shards(): pl.pallas_call(kernel, out_shape=(jax.ShapeDtypeStruct((1, 16), jnp.float...]
    all_gather x1 -> x0, waiting for transfers between devices: 52.3 us -> none  [shards(): lax.all_gather(hidden_states, DP, axis=0, tiled=True)]
    all_gather x4 -> x0, blocking collectives: 38.1 us -> none  [collected_together(): both, at, found = (lax.all_gather(jnp.concatenate(lines), axis), 0, {})]
    unnamed x1 -> x0, blocking collectives: 25.4 us -> none
    dot_general x1 -> x0, matrix products: 16.8 us -> none  [shards(): logits = jnp.dot(states, out_weight, preferred_element_type=jnp.float32)]
    reduce_sum x2 -> x0, other arithmetic: 2.72 us -> none  [the longest x1 2.09 us: shards(): exp_local = jnp.sum(jnp.exp(logits - local_top[:, None]), axis=1)]
  transfers between devices with their start and end apart: 1 -> 0, of which waited for: 1 -> 0; matrix products, arithmetic and copies ran while one was open for 1% -> 0% of each run, Pallas kernels for 0% -> 0%
where the time goes in v1:
time: 56.4 us; the launch traced here: 56.3 us
  Pallas kernels  52.8 us (94%)
  between operations  2.4 us (4%)
  local copies, waits for them, and re-layouts  1.11 us (2%)
    pallas_call x1, Pallas kernels, shards(): pl.pallas_call(kernel, out_shape=(jax.ShapeDtypeStruct((1, 16), jnp.float...  52.8 us

profile of v1, /device:TPU:0, one launch (start us, length us, event | category | flops | bytes accessed | tf_op | source)
XLA Modules:
  0.0 56.3 jit_solution(11642627562400003586)
XLA Ops:
  0.6 52.8 %score.1 = (f32[1,16]{1,0:T(1,128)}, f32[1,1]{1,0:T(1,128)}) custom-call(bf16[16,3584]{1,0:T(8,128)(2,1)} %h_ref.1, s32[16]{0:T(128)} %t_ref.1, bf16[3584,1536]{1,0:T(8,128)(2,1)} %w_ref.1), custom_call_target="tpu_custom_call" | custom-call | tf_op jit(solution)/shard_map/score/pallas_call | solution.py:331
  53.4 1.1 %copy.7 = f32[16]{0:T(128)} copy(f32[16]{0:T(128)} %bitcast.2) | data formatting | bytes 128

commit v2 on v1

--- a/solution.py
+++ b/solution.py
@@ -16,13 +16,13 @@
 STARTS = (0, 768, 1280)
 HALF = 1792
 ROWS = (
-    (0, 0), (0, 1), (0, 2), (0, 3),
+    (0, 0), (0, 1), (0, 3), (0, 2),
     (3, 0), (1, 0),
     (3, 1), (1, 3),
-    (2, 0), (1, 2),
-    (3, 2), (2, 3),
+    (3, 3), (1, 2),
+    (3, 2), (1, 1),
+    (2, 0), (2, 3),
     (2, 1), (2, 2),
-    (3, 3), (1, 1),
 )
 SLOT = {row: i for i, row in enumerate(ROWS)}
 NT = 512
@@ -49,12 +49,16 @@
 
     partner = pos + (1 - core,)
 
+    def columns(j, h):
+        return pl.ds(pl.multiple_of(h * HALF + STARTS[j], 256), WIDTHS[j])
+
     loads = []
     for j in range(3):
         for k, (buf, h) in enumerate(((own[j], core), (part[j], 1 - core))):
-            cols = pl.ds(pl.multiple_of(h * HALF + STARTS[j], 256), WIDTHS[j])
             loads.append(
-                pltpu.make_async_copy(h_ref.at[:, cols], buf.at[pl.ds(0, 16)], local.at[2 * j + k])
+                pltpu.make_async_copy(
+                    h_ref.at[:, columns(j, h)], buf.at[pl.ds(0, 16)], local.at[2 * j + k]
+                )
             )
     loads.append(pltpu.make_async_copy(t_ref, tsm, local.at[6]))
     for copy in loads:
@@ -72,6 +76,7 @@
 
     barrier = pltpu.get_barrier_semaphore()
     peers = [partner] + [along(k, s) for k in range(3) for s in (1, 2, 3)]
+    peers += [along(2, s)[:3] + (1 - core,) for s in (1, 2, 3)]
     for peer in peers:
         pl.semaphore_signal(barrier, inc=1, device_id=peer, device_id_type=MESH)
     pl.semaphore_wait(barrier, len(peers))
@@ -87,13 +92,13 @@
 
     def a_copy(j, s):
         return remote(
-            own[j].at[pl.ds(0, 16)], own[j].at[pl.ds((4 - s) * 16, 16)],
+            h_ref.at[:, columns(j, core)], own[j].at[pl.ds((4 - s) * 16, 16)],
             a_send.at[j, s - 1], a_recv.at[j, 3 - s], moved(j + 2, s),
         )
 
     def b_copy(j, s):
         return remote(
-            block(own[j], 0), block(own[j], 4 - s),
+            block(own[j], 0), block(own[j], SLOT[0, 4 - s]),
             b_send.at[j, s - 1], b_recv.at[j, 3 - s], moved(j + 1, s),
         )
 
@@ -111,7 +116,7 @@
         ).wait_recv()
 
     def p_copy(j, k):
-        start, size = ((16, 48), (64, 192))[k] if k < 2 else (k * 128, 128)
+        start, size = {0: (16, 48), 8: (64, 128), 1: (192, 64)}.get(k, (k * 128, 128))
         return remote(
             own[j].at[pl.ds(start, size)], part[j].at[pl.ds(start, size)],
             p_send.at[j, k], p_recv.at[j, k], partner,
@@ -134,11 +139,11 @@
             tg.at[rows], tg.at[rows], t_send.at[k, 0], t_recv.at[k, r - 1], partner
         ).wait_recv()
 
+    for j in range(3):
+        for s in (1, 3, 2):
+            a_copy(j, s).start()
     for copy in loads:
         copy.wait()
-    for j in range(3):
-        for s in (1, 3, 2):
-            a_copy(j, s).start()
     spots = lax.broadcasted_iota(jnp.int32, (1, 128), 1) - lax.rem(chip, 8) * 16
     mine = jnp.zeros((1, 128), jnp.int32)
     for i in range(16):
@@ -151,11 +156,13 @@
     for j in range(3):
         for r in (1, 3, 2):
             a_copy(j, 4 - r).wait_recv()
-        for s in (1, 3, 2):
+        for s in (3, 1):
             b_copy(j, s).start()
+        p_copy(j, 0).start()
+    for j in range(3):
+        b_copy(j, 2).start()
         for s in (1, 3):
             c_copy(j, 0, 0, s).start()
-        p_copy(j, 0).start()
     for r in (1, 2, 3):
         t_wait(2, r)
     for s in (1, 3, 2):
@@ -163,79 +170,88 @@
     for copy in wloads:
         copy.wait()
 
-    def pair(p):
+    def pair(p, bufs, h):
         def entry(i, which):
             return sum(ROWS[2 * k + i][which] * (p == k).astype(jnp.int32) for k in range(8))
 
-        rel = [(entry(i, 0), entry(i, 1)) for i in range(2)]
-        for bufs, h in ((own, core), (part, 1 - core)):
-            for j in range(3):
-                spread = []
+        rel = [ROWS[2 * p + i] if isinstance(p, int) else (entry(i, 0), entry(i, 1)) for i in range(2)]
+        for j in range(3):
+            here = [sum(turn(h, j + d, k) * pos[k] for k in range(3)) for d in range(3)]
+            size = [sum(turn(h, j + d, k) * 16 * 4 ** (2 - k) for k in range(3)) for d in range(3)]
+            heads = [
+                lax.rem(here[0] + rc, 4) * size[0] + lax.rem(here[1] + rb, 4) * size[1]
+                for rc, rb in rel
+            ]
+            tails = [lax.rem(here[2] + r, 4) * size[2] for r in range(4)]
+            spread = [pl.multiple_of(head + tail, 16) for head in heads for tail in tails]
+            lhs = bufs[j][pl.ds(p * 128 if isinstance(p, int) else pl.multiple_of(p * 128, 128), 128), :]
+            rows = columns(j, h)
+            for n in range(vocab_cols // NT):
+                cols = pl.ds(n * NT, NT)
+                out = jnp.dot(lhs, w[rows, cols], preferred_element_type=jnp.float32)
                 for i in range(8):
-                    rc, rb = rel[i // 4]
-                    place = 0
-                    for k in range(3):
-                        shift = rc * turn(h, j, k) + rb * turn(h, j + 1, k)
-                        shift = shift + (i % 4) * turn(h, j + 2, k)
-                        place = place * 4 + lax.rem(pos[k] + shift, 4)
-                    spread.append(pl.multiple_of(place * 16, 16))
-                lhs = bufs[j][pl.ds(pl.multiple_of(p * 128, 128), 128), :]
-                rows = pl.ds(pl.multiple_of(h * HALF + STARTS[j], 256), WIDTHS[j])
-                for n in range(vocab_cols // NT):
-                    cols = pl.ds(n * NT, NT)
-                    out = jnp.dot(lhs, w[rows, cols], preferred_element_type=jnp.float32)
-                    for i in range(8):
-                        acc[pl.ds(spread[i], 16), cols] += out[16 * i : 16 * i + 16]
+                    acc[pl.ds(spread[i], 16), cols] += out[16 * i : 16 * i + 16]
+
+    def first_blocks():
+        for j in range(3):
+            for r in (1, 3):
+                b_copy(j, 4 - r).wait_recv()
+            c_copy(j, 0, 1, 1).start()
+            c_copy(j, 0, 3, 3).start()
+            c_copy(j, 0, 3, 1).start()
+            p_copy(j, 8).start()
 
     def step(p, carry):
-        @pl.when(p == 0)
+        @pl.when(p == 1)
         def _():
             for j in range(3):
-                for r in (1, 3, 2):
-                    b_copy(j, 4 - r).wait_recv()
-                c_copy(j, 0, 1, 1).start()
-                c_copy(j, 0, 3, 3).start()
+                b_copy(j, 2).wait_recv()
                 c_copy(j, 0, 2, 3).start()
+                c_copy(j, 0, 2, 1).start()
+                c_copy(j, 0, 1, 3).start()
                 p_copy(j, 1).start()
             for j in range(3):
                 p_copy(j, 0).wait_recv()
-                p_copy(j, 1).wait_recv()
-
-        for k in range(1, 7):
-
-            @pl.when(p == k)
+                p_copy(j, 8).wait_recv()
+
+        for k in range(2, 8):
+
+            @pl.when(p == (k - 1 if k in (3, 4) else k))
             def _(k=k):
                 for j in range(3):
-                    c_wait(j, 2 * k + 2)
-                    c_wait(j, 2 * k + 3)
-                    if k == 1:
+                    c_wait(j, 2 * k)
+                    c_wait(j, 2 * k + 1)
+                    if k == 2:
                         c_copy(j, 3, 0, 1).start()
-                        c_copy(j, 0, 2, 1).start()
-                    if k == 2:
+                    if k == 3:
                         c_copy(j, 3, 1, 1).start()
                         c_copy(j, 1, 3, 3).start()
-                        c_copy(j, 0, 3, 1).start()
-                    if k == 3:
+                    if k == 4:
                         c_copy(j, 1, 2, 3).start()
-                        c_copy(j, 0, 1, 3).start()
-                    p_copy(j, k + 1).start()
-                if k == 1:
+                    p_copy(j, k).start()
+                if k == 2:
                     for r in (1, 2, 3):
                         t_wait(1, r)
                     for s in (1, 3, 2):
                         t_copy(0, s).start()
 
-        for k in range(2, 8):
-
-            @pl.when(p == k)
+        for k in range(1, 7):
+
+            @pl.when(p == k + 1)
             def _(k=k):
                 for j in range(3):
                     p_copy(j, k).wait_recv()
 
-        pair(p)
+        pair(p - 1, part, 1 - core)
+        pair(p, own, core)
         return carry
 
-    lax.fori_loop(0, 8, step, 0)
+    first_blocks()
+    pair(0, own, core)
+    lax.fori_loop(1, 8, step, 0)
+    for j in range(3):
+        p_copy(j, 7).wait_recv()
+    pair(7, part, 1 - core)
     for r in (1, 2, 3):
         t_wait(0, r)
 
@@ -260,7 +276,7 @@
             for n in range(vocab_cols // 128):
                 x = acc[rows, n * 128 : n * 128 + 128]
                 total = total + jnp.exp(x - top)
-                hit = hit + jnp.where(ahead == float(n * 128), x, 0.0)
+                hit = jnp.where(ahead == float(n * 128), x, hit)
             lanes[0, there, :] = top
             lanes[1, there, :] = total
             lanes[2, there, :] = hit
@@ -275,34 +291,48 @@
 
     def joined(found):
         top = functools.reduce(jnp.maximum, [f[0] for f in found])
-        total = sum(f[1] * jnp.exp(f[0] - top) for f in found)
-        return top, total, sum(f[2] for f in found)
-
-    now = tuple(stats[0, k] for k in range(3))
-    for phase, (axis, size) in enumerate(((3, 2), (2, 4), (1, 4), (0, 4))):
-        at = core if axis == 3 else pos[axis]
-        for k in range(3):
+        total = sum(jnp.exp(f[0] - top) for f in found)
+        return top + jnp.log(total), sum(f[1] for f in found)
+
+    now = (stats[0, 0] + jnp.log(stats[0, 1]), stats[0, 2])
+    for phase, axis in enumerate((2, 1, 0)):
+        cores = (0, 1) if phase == 0 else (0,)
+        size = 4 * len(cores)
+        at = pos[axis] * len(cores) + (core if phase == 0 else 0)
+        for k in range(2):
             parts[phase, at, k] = now[k]
         copies = []
-        for s in range(1, size):
-            to = partner if axis == 3 else along(axis, s)
-            copies.append(
+        for s in (1, 3, 2, 0):
+            for other in cores:
+                if s == 0 and other == 0:
+                    continue
+                to = along(axis, s)
+                to = to[:3] + (lax.rem(core + other, 2),)
+                n = s * len(cores) + other
+                back = (4 - s) % 4 * len(cores) + other
+                copies.append(
+                    remote(
+                        parts.at[phase, at], parts.at[phase, at],
+                        s_send.at[phase, n], s_recv.at[phase, back], to,
+                    )
+                )
+                copies[-1].start()
+        for s in range(4):
+            for other in cores:
+                if s == 0 and other == 0:
+                    continue
+                there = lax.rem(pos[axis] + s, 4) * len(cores)
+                if phase == 0:
+                    there = there + lax.rem(core + other, 2)
+                n = s * len(cores) + other
                 remote(
-                    parts.at[phase, at], parts.at[phase, at],
-                    s_send.at[phase, s - 1], s_recv.at[phase, size - 1 - s], to,
-                )
-            )
-            copies[-1].start()
-        for s in range(1, size):
-            other = lax.rem(at + s, size)
-            remote(
-                parts.at[phase, other], parts.at[phase, other],
-                s_send.at[phase, s - 1], s_recv.at[phase, s - 1], partner,
-            ).wait_recv()
-        now = joined([tuple(parts[phase, q, k] for k in range(3)) for q in range(size)])
+                    parts.at[phase, there], parts.at[phase, there],
+                    s_send.at[phase, n], s_recv.at[phase, n], partner,
+                ).wait_recv()
+        now = joined([tuple(parts[phase, q, k] for k in range(2)) for q in range(size)])
         for copy in copies:
             copy.wait_send()
-    loss = now[0] + jnp.log(now[1]) - now[2]
+    loss = now[0] - now[1]
     mean_ref[0, 0] = jnp.sum(loss) / loss.size
     stats[0, 0] = loss
     row = stats[0, 0, pl.ds(chip // 8, 1), :]
@@ -318,7 +348,7 @@
                 block(own[j], slot), block(own[j], slot),
                 c_send.at[j, slot - 4], c_recv.at[j, slot - 4], partner,
             ).wait_send()
-        for k in range(8):
+        for k in range(9):
             p_copy(j, k).wait_send()
     for k in range(3):
         for s in (1, 2, 3):
@@ -347,11 +377,11 @@
             pltpu.SMEM((16,), jnp.int32),
             pltpu.VMEM((1, 3, 8, 128), jnp.float32),
             pltpu.VMEM((3, 128, 128), jnp.float32),
-            pltpu.VMEM((4, 4, 3, 8, 128), jnp.float32),
+            pltpu.VMEM((3, 8, 2, 8, 128), jnp.float32),
             pltpu.VMEM((128, 128), jnp.float32),
             dma((3, 3)), dma((3, 3)), dma((3, 3)), dma((3, 3)),
-            dma((3, 12)), dma((3, 12)), dma((3, 8)), dma((3, 8)),
-            dma((3, 3)), dma((3, 3)), dma((4, 3)), dma((4, 3)),
+            dma((3, 12)), dma((3, 12)), dma((3, 9)), dma((3, 9)),
+            dma((3, 3)), dma((3, 3)), dma((3, 8)), dma((3, 8)),
             dma((7,)), dma((7,)),
         ],
         compiler_params=pltpu.CompilerParams(

time: 56.4 us -> 52.1 us (0.924)
  Pallas kernels: 52.8 us -> 48.4 us
    pallas_call x1, Pallas kernels: 52.8 us -> 48.4 us  [shards(): pl.pallas_call(kernel, out_shape=(jax.ShapeDtypeStruct((1, 16), jnp.float...]
where the time goes in v2:
time: 52.1 us; the launch traced here: 51.9 us
  Pallas kernels  48.4 us (93%)
  between operations  2.4 us (5%)
  local copies, waits for them, and re-layouts  1.11 us (2%)
    pallas_call x1, Pallas kernels, shards(): pl.pallas_call(kernel, out_shape=(jax.ShapeDtypeStruct((1, 16), jnp.float...  48.4 us
    unnamed x1, local copies, waits for them, and re-layouts  1.11 us

profile of v2, /device:TPU:0, one launch (start us, length us, event | category | flops | bytes accessed | tf_op | source)
XLA Modules:
  0.0 51.9 jit_solution(4801419441102461799)
XLA Ops:
  0.6 48.4 %score.1 = (f32[1,16]{1,0:T(1,128)}, f32[1,1]{1,0:T(1,128)}) custom-call(bf16[16,3584]{1,0:T(8,128)(2,1)} %h_ref.1, s32[16]{0:T(128)} %t_ref.1, bf16[3584,1536]{1,0:T(8,128)(2,1)} %w_ref.1), custom_call_target="tpu_custom_call" | custom-call | tf_op jit(solution)/shard_map/score/pallas_call | solution.py:361
  49.1 1.1 %copy.7 = f32[16]{0:T(128)} copy(f32[16]{0:T(128)} %bitcast.2) | data formatting | bytes 128

commit v3 on v2

--- a/solution.py
+++ b/solution.py
@@ -16,11 +16,12 @@
 STARTS = (0, 768, 1280)
 HALF = 1792
 ROWS = (
-    (0, 0), (0, 1), (0, 3), (0, 2),
+    (0, 0), (0, 1),
     (3, 0), (1, 0),
+    (0, 3), (0, 2),
     (3, 1), (1, 3),
-    (3, 3), (1, 2),
-    (3, 2), (1, 1),
+    (3, 3), (1, 1),
+    (3, 2), (1, 2),
     (2, 0), (2, 3),
     (2, 1), (2, 2),
 )
@@ -28,7 +29,7 @@
 NT = 512
 
 
-def kernel(h_ref, t_ref, w_ref, loss_ref, mean_ref, *scratch):
+def kernel(h_ref, t_ref, w_ref, norm_ref, hit_ref, mean_ref, *scratch):
     own, part = scratch[0:3], scratch[3:6]
     (w, acc, tg, tsm, stats, lanes, parts, line,
      a_send, a_recv, b_send, b_recv, c_send, c_recv, p_send, p_recv,
@@ -106,17 +107,17 @@
         src, dst = SLOT[rc, rb], SLOT[(rc - s) % 4, rb]
         return remote(
             block(own[j], src), block(own[j], dst),
-            c_send.at[j, dst - 4], c_recv.at[j, dst - 4], moved(j, s),
+            c_send.at[j, dst], c_recv.at[j, dst], moved(j, s),
         )
 
     def c_wait(j, slot):
         remote(
             block(own[j], slot), block(own[j], slot),
-            c_send.at[j, slot - 4], c_recv.at[j, slot - 4], partner,
+            c_send.at[j, slot], c_recv.at[j, slot], partner,
         ).wait_recv()
 
     def p_copy(j, k):
-        start, size = {0: (16, 48), 8: (64, 128), 1: (192, 64)}.get(k, (k * 128, 128))
+        start, size = {0: (16, 48), 8: (64, 64)}.get(k, (k * 128, 128))
         return remote(
             own[j].at[pl.ds(start, size)], part[j].at[pl.ds(start, size)],
             p_send.at[j, k], p_recv.at[j, k], partner,
@@ -159,8 +160,12 @@
         for s in (3, 1):
             b_copy(j, s).start()
         p_copy(j, 0).start()
+    for j in (1, 2):
+        for s in (1, 3):
+            c_copy(j, 0, 0, s).start()
     for j in range(3):
         b_copy(j, 2).start()
+    for j in (0,):
         for s in (1, 3):
             c_copy(j, 0, 0, s).start()
     for r in (1, 2, 3):
@@ -193,40 +198,40 @@
                     acc[pl.ds(spread[i], 16), cols] += out[16 * i : 16 * i + 16]
 
     def first_blocks():
-        for j in range(3):
+        for j in (1, 2, 0):
             for r in (1, 3):
                 b_copy(j, 4 - r).wait_recv()
             c_copy(j, 0, 1, 1).start()
             c_copy(j, 0, 3, 3).start()
             c_copy(j, 0, 3, 1).start()
+            c_copy(j, 0, 1, 3).start()
             p_copy(j, 8).start()
 
     def step(p, carry):
         @pl.when(p == 1)
         def _():
             for j in range(3):
-                b_copy(j, 2).wait_recv()
-                c_copy(j, 0, 2, 3).start()
-                c_copy(j, 0, 2, 1).start()
-                c_copy(j, 0, 1, 3).start()
-                p_copy(j, 1).start()
-            for j in range(3):
                 p_copy(j, 0).wait_recv()
                 p_copy(j, 8).wait_recv()
 
-        for k in range(2, 8):
-
-            @pl.when(p == (k - 1 if k in (3, 4) else k))
+        for k in range(1, 8):
+
+            @pl.when(p == k)
             def _(k=k):
                 for j in range(3):
-                    c_wait(j, 2 * k)
-                    c_wait(j, 2 * k + 1)
                     if k == 2:
+                        b_copy(j, 2).wait_recv()
+                        c_copy(j, 0, 2, 3).start()
+                        c_copy(j, 0, 2, 1).start()
+                    else:
+                        c_wait(j, 2 * k)
+                        c_wait(j, 2 * k + 1)
+                    if k == 1:
                         c_copy(j, 3, 0, 1).start()
                     if k == 3:
                         c_copy(j, 3, 1, 1).start()
                         c_copy(j, 1, 3, 3).start()
-                    if k == 4:
+                    if k == 5:
                         c_copy(j, 1, 2, 3).start()
                     p_copy(j, k).start()
                 if k == 2:
@@ -259,11 +264,11 @@
     lane = lax.broadcasted_iota(jnp.int32, (128, 128), 1).astype(jnp.float32)
     base = lane + first.astype(jnp.float32)
 
-    def tokens(i, carry):
+    def tokens(i, u):
         wanted = jnp.zeros((1, 128), jnp.int32)
         for k in range(8):
             wanted = wanted + tg[i * 8 + k]
-        line[...] = jnp.broadcast_to(wanted.astype(jnp.float32), (128, 128)).T - base
+        line[u] = jnp.broadcast_to(wanted.astype(jnp.float32), (128, 128)).T - base
         for half in range(2):
             rows = pl.ds(pl.multiple_of(i * 128 + half * 64, 64), 64)
             there = pl.ds(half * 64, 64)
@@ -272,22 +277,26 @@
                 top = jnp.maximum(top, acc[rows, n * 128 : n * 128 + 128])
             total = jnp.zeros((64, 128), jnp.float32)
             hit = jnp.zeros((64, 128), jnp.float32)
-            ahead = line[there, :]
+            ahead = line[u, there, :]
             for n in range(vocab_cols // 128):
                 x = acc[rows, n * 128 : n * 128 + 128]
                 total = total + jnp.exp(x - top)
                 hit = jnp.where(ahead == float(n * 128), x, hit)
-            lanes[0, there, :] = top
-            lanes[1, there, :] = total
-            lanes[2, there, :] = hit
-        top = lanes[0].T
+            lanes[u, 0, there, :] = top
+            lanes[u, 1, there, :] = total
+            lanes[u, 2, there, :] = hit
+        top = lanes[u, 0].T
         best = jnp.max(top, axis=0, keepdims=True)
         stats[0, 0, pl.ds(i, 1), :] = best
-        stats[0, 1, pl.ds(i, 1), :] = jnp.sum(lanes[1].T * jnp.exp(top - best), axis=0, keepdims=True)
-        stats[0, 2, pl.ds(i, 1), :] = jnp.sum(lanes[2].T, axis=0, keepdims=True)
+        stats[0, 1, pl.ds(i, 1), :] = jnp.sum(lanes[u, 1].T * jnp.exp(top - best), axis=0, keepdims=True)
+        stats[0, 2, pl.ds(i, 1), :] = jnp.sum(lanes[u, 2].T, axis=0, keepdims=True)
+
+    def token_pair(i, carry):
+        for u in range(2):
+            tokens(2 * i + u, u)
         return carry
 
-    lax.fori_loop(0, 8, tokens, 0)
+    lax.fori_loop(0, 4, token_pair, 0)
 
     def joined(found):
         top = functools.reduce(jnp.maximum, [f[0] for f in found])
@@ -332,21 +341,21 @@
         now = joined([tuple(parts[phase, q, k] for k in range(2)) for q in range(size)])
         for copy in copies:
             copy.wait_send()
-    loss = now[0] - now[1]
-    mean_ref[0, 0] = jnp.sum(loss) / loss.size
-    stats[0, 0] = loss
-    row = stats[0, 0, pl.ds(chip // 8, 1), :]
-    row = pltpu.roll(row, lax.rem(128 - lax.rem(chip, 8) * 16, 128), 1)
-    loss_ref[...] = row[:, 0:16]
+    mean_ref[0, 0] = jnp.sum(now[0] - now[1]) / now[0].size
+    for k, out in enumerate((norm_ref, hit_ref)):
+        stats[0, k] = now[k]
+        row = stats[0, k, pl.ds(chip // 8, 1), :]
+        row = pltpu.roll(row, lax.rem(128 - lax.rem(chip, 8) * 16, 128), 1)
+        out[...] = row[:, 0:16]
 
     for j in range(3):
         for s in (1, 2, 3):
             a_copy(j, s).wait_send()
             b_copy(j, s).wait_send()
-        for slot in range(4, 16):
+        for slot in (2, 3, *range(6, 16)):
             remote(
                 block(own[j], slot), block(own[j], slot),
-                c_send.at[j, slot - 4], c_recv.at[j, slot - 4], partner,
+                c_send.at[j, slot], c_recv.at[j, slot], partner,
             ).wait_send()
         for k in range(9):
             p_copy(j, k).wait_send()
@@ -358,14 +367,16 @@
 def shards(hidden_states, targets, out_weight):
     depth, cols = out_weight.shape
     dma = pltpu.SemaphoreType.DMA
-    loss, mean = pl.pallas_call(
+    log_norm, picked, mean = pl.pallas_call(
         kernel,
         out_shape=(
+            jax.ShapeDtypeStruct((1, 16), jnp.float32),
             jax.ShapeDtypeStruct((1, 16), jnp.float32),
             jax.ShapeDtypeStruct((1, 1), jnp.float32),
         ),
         in_specs=[pl.BlockSpec(memory_space=pl.ANY)] * 3,
         out_specs=(
+            pl.BlockSpec(memory_space=pltpu.VMEM),
             pl.BlockSpec(memory_space=pltpu.VMEM),
             pl.BlockSpec(memory_space=pltpu.SMEM),
         ),
@@ -376,11 +387,11 @@
             pltpu.VMEM((64, 1, 128), jnp.int32),
             pltpu.SMEM((16,), jnp.int32),
             pltpu.VMEM((1, 3, 8, 128), jnp.float32),
-            pltpu.VMEM((3, 128, 128), jnp.float32),
+            pltpu.VMEM((2, 3, 128, 128), jnp.float32),
             pltpu.VMEM((3, 8, 2, 8, 128), jnp.float32),
-            pltpu.VMEM((128, 128), jnp.float32),
+            pltpu.VMEM((2, 128, 128), jnp.float32),
             dma((3, 3)), dma((3, 3)), dma((3, 3)), dma((3, 3)),
-            dma((3, 12)), dma((3, 12)), dma((3, 9)), dma((3, 9)),
+            dma((3, 16)), dma((3, 16)), dma((3, 9)), dma((3, 9)),
             dma((3, 3)), dma((3, 3)), dma((3, 8)), dma((3, 8)),
             dma((7,)), dma((7,)),
         ],
@@ -389,7 +400,7 @@
         ),
         name="score",
     )(hidden_states, targets, out_weight)
-    return loss.reshape(16), mean.reshape(())
+    return (log_norm - picked).reshape(16), mean.reshape(())
 
 
 def solution(mesh):

time: 52.1 us -> 51.6 us (level)
  other arithmetic: 0 us -> 1.15 us
  local copies, waits for them, and re-layouts: 1.11 us -> 0 us
    reshape x0 -> x1, other arithmetic: none -> 1.15 us  [shards(): return ((log_norm - picked).reshape(16), mean.reshape(()))]
    unnamed x1 -> x0, local copies, waits for them, and re-layouts: 1.11 us -> none
where the time goes in v3:
time: 51.6 us; the launch traced here: 51.5 us
  Pallas kernels  47.9 us (93%)
  between operations  2.4 us (5%)
  other arithmetic  1.15 us (2%)
    pallas_call x1, Pallas kernels, shards(): pl.pallas_call(kernel, out_shape=(jax.ShapeDtypeStruct((1, 16), jnp.float...  47.9 us
    reshape x1, other arithmetic, shards(): return ((log_norm - picked).reshape(16), mean.reshape(()))  1.15 us

profile of v3, /device:TPU:0, one launch (start us, length us, event | category | flops | bytes accessed | tf_op | source)
XLA Modules:
  0.0 51.5 jit_solution(13344695722476588794)
XLA Ops:
  0.6 47.9 %score.1 = (f32[1,16]{1,0:T(1,128)}, f32[1,16]{1,0:T(1,128)}, f32[1,1]{1,0:T(1,128)}) custom-call(bf16[16,3584]{1,0:T(8,128)(2,1)} %h_ref.1, s32[16]{0:T(128)} %t_ref.1, bf16[3584,1536]{1,0:T(8,128)(2,1)} %w_ref.1), custom_call_target="tpu_custom_call" | custom-call | tf_op jit(solution)/shard_map/score/pallas_call | solution.py:370
  48.6 1.1 %subtract_bitcast_fusion = f32[16]{0:T(128)} fusion(f32[1,16]{1,0:T(1,128)} %get-tuple-element.5, f32[1,16]{1,0:T(1,128)} %get-tuple-element.6), kind=kLoop, calls=%fused_computation | loop fusion | flops 16 | bytes 192 | tf_op jit(solution)/shard_map/reshape | solution.py:403
